TPU v7x, 512 devices: a whole 4x8x8 slice. The times are simulated.
512 devices in a mesh: space: 64 (over z, x, y_lo), sta: 8 (over y_hi, core).
Axes of the slice: x: 4, y: 8 (y_hi: 4, y_lo: 2; y = y_hi * 2 + y_lo), z: 8, core: 2. Of those that a mesh axis runs over, the one named last changes fastest.
Arguments:
- coarse_times: float32 [16, 320, 32, 128], P('sta', 'space'), as said below
- model_map: int32 [320, 32, 128], P('space'), may hold values from 0 to 63
- slowness: float32 [64], replicated, may hold values from 0.12 to 0.3
- picks: float32 [256, 16], replicated
- pick_mask: int32 [256, 16], replicated, may hold values from 0 to 1, as said below
Outputs:
- refined: float32 [16, 320, 32, 128], P(None, 'space', 'sta')
- density: float32 [256, 320, 32, 128], P(None, 'space', 'sta')
Inputs may be any that keep to these rules, and one draw needn't show every extreme that they name: `pick_mask`: each event has at least 4 stations with a pick. `coarse_times`: zero at each station's own cell and positive elsewhere.
All inputs are finite; a program needn't handle non-finite values.
Results may differ from a plain program's by a relative error of at most 0.0003.
Values sent between devices are 32-bit elements; how exact they have to be, the bound alone decides.
A program may use at most 64 MiB of HBM per device.

v0:
```python
import jax
import jax.numpy as jnp
from jax import lax
from jax.sharding import PartitionSpec as P

ROUNDS = 12
BIG = 1000000.0
pick_sigma = 0.25
grid_step = 1.0
block_events = 32


def extended_2(block, sides, width):
    for axis, dim in sides:
        count = lax.axis_size(axis)
        forward = [(i, i + 1) for i in range(count - 1)]
        backward = [(target, source) for source, target in forward]
        low = lax.ppermute(
            lax.slice_in_dim(block, block.shape[dim] - width, None, axis=dim), axis, forward
        )
        high = lax.ppermute(lax.slice_in_dim(block, 0, width, axis=dim), axis, backward)
        block = jnp.concatenate([low, block, high], axis=dim)
    return block


def godunov(near_one, near_two, near_three, speed):
    lowest = jnp.minimum(jnp.minimum(near_one, near_two), near_three)
    highest = jnp.maximum(jnp.maximum(near_one, near_two), near_three)
    middle = jnp.maximum(
        jnp.minimum(near_one, near_two), jnp.minimum(jnp.maximum(near_one, near_two), near_three)
    )
    gap_mid = middle - lowest
    gap_high = highest - lowest
    two_sided = 0.5 * (
        gap_mid + jnp.sqrt(jnp.maximum(2.0 * speed * speed - gap_mid * gap_mid, 0.0))
    )
    gap_sum = gap_mid + gap_high
    squares = gap_mid * gap_mid + gap_high * gap_high - speed * speed
    three_sided = (gap_sum + jnp.sqrt(jnp.maximum(gap_sum * gap_sum - 3.0 * squares, 0.0))) / 3.0
    increase = jnp.where(
        speed <= gap_mid, speed, jnp.where(two_sided <= gap_high, two_sided, three_sided)
    )
    return lowest + increase


def relax(extended, speed):
    centre = extended[:, 1:-1]
    along_x = jnp.minimum(extended[:, :-2], extended[:, 2:])
    padded = jnp.pad(centre, ((0, 0), (0, 0), (1, 1), (1, 1)), constant_values=BIG)
    along_y = jnp.minimum(padded[:, :, :-2, 1:-1], padded[:, :, 2:, 1:-1])
    along_z = jnp.minimum(padded[:, :, 1:-1, :-2], padded[:, :, 1:-1, 2:])
    return jnp.minimum(centre, godunov(along_x, along_y, along_z, speed[None]))


def close_rims(extended, rim_width, at_lower, at_upper):
    cell_count = extended.shape[1]
    position = lax.broadcasted_iota(jnp.int32, (1, cell_count, 1, 1), 1)
    outside = (position < rim_width) & at_lower | (position >= cell_count - rim_width) & at_upper
    return jnp.where(outside, BIG, extended)


def misfit_block(event_pair, flat_tables):
    arrivals, observed = event_pair
    pick_count = jnp.sum(observed, 1)
    residual = arrivals[:, :, None] - flat_tables[None]
    anchor_shift = jnp.sum(observed[:, :, None] * residual, 1) / pick_count[:, None]
    deviation = residual - anchor_shift[:, None, :]
    return jnp.sum(observed[:, :, None] * deviation * deviation, 1)


def body(coarse_times, model_map, slowness, picks, pick_mask):
    levels = lax.broadcasted_iota(jnp.int32, (slowness.shape[0], 1, 1, 1), 0)
    speed = grid_step * jnp.sum(
        jnp.where(model_map[None] == levels, slowness[:, None, None, None], 0.0), 0
    )
    position_space = lax.axis_index("space")
    devices_space = lax.axis_size("space")
    at_lower = position_space == 0
    at_upper = position_space == devices_space - 1
    tables = coarse_times

    def one_round(round_index, tables):
        extended = extended_2(tables, (("space", 1),), 1)
        return relax(close_rims(extended, 1, at_lower, at_upper), speed)

    tables = lax.fori_loop(0, ROUNDS, one_round, tables)
    refined = lax.all_to_all(tables, "sta", split_axis=2, concat_axis=0, tiled=True)
    stations = refined.shape[0]
    flat_tables = refined.reshape(stations, -1)
    observed = pick_mask.astype(jnp.float32)
    blocks = lax.map(
        lambda event_pair: misfit_block(event_pair, flat_tables),
        (picks.reshape(-1, block_events, stations), observed.reshape(-1, block_events, stations)),
    )
    score = -0.5 * blocks.reshape(picks.shape[0], -1) / (pick_sigma * pick_sigma)
    local_top = jnp.max(score, 1)
    top_score = lax.pmax(local_top, ("space", "sta"))
    cell_weights = jnp.exp(score - top_score[:, None])
    mass_sum = lax.psum(jnp.sum(cell_weights, 1), ("space", "sta"))
    density = cell_weights / mass_sum[:, None]
    density = density.reshape(picks.shape[0], refined.shape[1], refined.shape[2], refined.shape[3])
    return (refined, density)


def solution(mesh):
    placed = (P("sta", "space", None, None), P("space", None, None), P(), P(), P())
    return jax.shard_map(
        body,
        mesh=mesh,
        in_specs=placed,
        out_specs=(P(None, "space", "sta", None), P(None, "space", "sta", None)),
        check_vma=False,
    )
```

profile of v0, /device:TPU:1, one launch (start us, length us, event | category | flops | bytes accessed | tf_op | source)
XLA Modules:
  0.0 400.3 jit_solution(15108687910519187585)
XLA Ops:
  1.5 1.5 select_reduce_fusion
  3.1 96.4 %while.22 = (s32[]{:T(128)}, f32[2,5,32,128]{3,2,1,0:T(8,128)S(1)}, pred[]{:T(512)}, pred[]{:T(512)}, f32[5,32,128]{2,1,0:T(8,128)S(1)}, /*index=5*/f32[1,5,32,128]{3,2,1,0:T(8,128)S(1)}, s32[]{:T(128)}) while((s32[]{:T(128)}, f32[2,5,32,128]{3,2,1,0:T(8,128)S(1)}, pred[]{:T(512)}, pred[]{:T(512)}, f32[5,32,128]{2,1,0:T(8,128)S(1)}, ...), condition=%wide.region_2.3_spmd, body=%wide.region_1.2_spmd.sunk | while | flops 1523749 | bytes 2244781 | solution.py:86
  3.1 1.3 collective-permute-start
  4.4 4.6 %collective-permute-start.1 = (f32[2,1,32,128]{3,2,1,0:T(8,128)S(1)}, f32[2,1,32,128]{3,2,1,0:T(8,128)S(1)}, u32[]{:S(2)}, u32[]{:S(2)}) collective-permute-start(f32[2,1,32,128]{3,2,1,0:T(8,128)S(1)} %get-tuple-element.226), channel_id=1, source_target_pairs={{0,8},{8,16},{16,24},{24,32},{32,40},{40,48},{48,56},{56,64},{64,7... | collective-permute-start | bytes 98312 | tf_op jit(solution)/shard_map/while/body/eval_jaxpr/ppermute | solution.py:18
  10.6 1.3 collective-permute-start
  11.9 4.9 %collective-permute-start.1 = (f32[2,1,32,128]{3,2,1,0:T(8,128)S(1)}, f32[2,1,32,128]{3,2,1,0:T(8,128)S(1)}, u32[]{:S(2)}, u32[]{:S(2)}) collective-permute-start(f32[2,1,32,128]{3,2,1,0:T(8,128)S(1)} %get-tuple-element.226), channel_id=1, source_target_pairs={{0,8},{8,16},{16,24},{24,32},{32,40},{40,48},{48,56},{56,64},{64,7... | collective-permute-start | bytes 98312 | tf_op jit(solution)/shard_map/while/body/eval_jaxpr/ppermute | solution.py:18
  18.2 1.3 collective-permute-start
  19.5 5.2 %collective-permute-start.1 = (f32[2,1,32,128]{3,2,1,0:T(8,128)S(1)}, f32[2,1,32,128]{3,2,1,0:T(8,128)S(1)}, u32[]{:S(2)}, u32[]{:S(2)}) collective-permute-start(f32[2,1,32,128]{3,2,1,0:T(8,128)S(1)} %get-tuple-element.226), channel_id=1, source_target_pairs={{0,8},{8,16},{16,24},{24,32},{32,40},{40,48},{48,56},{56,64},{64,7... | collective-permute-start | bytes 98312 | tf_op jit(solution)/shard_map/while/body/eval_jaxpr/ppermute | solution.py:18
  26.2 1.3 collective-permute-start
  27.5 5.2 %collective-permute-start.1 = (f32[2,1,32,128]{3,2,1,0:T(8,128)S(1)}, f32[2,1,32,128]{3,2,1,0:T(8,128)S(1)}, u32[]{:S(2)}, u32[]{:S(2)}) collective-permute-start(f32[2,1,32,128]{3,2,1,0:T(8,128)S(1)} %get-tuple-element.226), channel_id=1, source_target_pairs={{0,8},{8,16},{16,24},{24,32},{32,40},{40,48},{48,56},{56,64},{64,7... | collective-permute-start | bytes 98312 | tf_op jit(solution)/shard_map/while/body/eval_jaxpr/ppermute | solution.py:18
  34.2 1.3 collective-permute-start
  35.5 5.2 %collective-permute-start.1 = (f32[2,1,32,128]{3,2,1,0:T(8,128)S(1)}, f32[2,1,32,128]{3,2,1,0:T(8,128)S(1)}, u32[]{:S(2)}, u32[]{:S(2)}) collective-permute-start(f32[2,1,32,128]{3,2,1,0:T(8,128)S(1)} %get-tuple-element.226), channel_id=1, source_target_pairs={{0,8},{8,16},{16,24},{24,32},{32,40},{40,48},{48,56},{56,64},{64,7... | collective-permute-start | bytes 98312 | tf_op jit(solution)/shard_map/while/body/eval_jaxpr/ppermute | solution.py:18
  42.1 1.3 collective-permute-start
  43.4 5.2 %collective-permute-start.1 = (f32[2,1,32,128]{3,2,1,0:T(8,128)S(1)}, f32[2,1,32,128]{3,2,1,0:T(8,128)S(1)}, u32[]{:S(2)}, u32[]{:S(2)}) collective-permute-start(f32[2,1,32,128]{3,2,1,0:T(8,128)S(1)} %get-tuple-element.226), channel_id=1, source_target_pairs={{0,8},{8,16},{16,24},{24,32},{32,40},{40,48},{48,56},{56,64},{64,7... | collective-permute-start | bytes 98312 | tf_op jit(solution)/shard_map/while/body/eval_jaxpr/ppermute | solution.py:18
  50.1 1.3 collective-permute-start
  51.4 5.2 %collective-permute-start.1 = (f32[2,1,32,128]{3,2,1,0:T(8,128)S(1)}, f32[2,1,32,128]{3,2,1,0:T(8,128)S(1)}, u32[]{:S(2)}, u32[]{:S(2)}) collective-permute-start(f32[2,1,32,128]{3,2,1,0:T(8,128)S(1)} %get-tuple-element.226), channel_id=1, source_target_pairs={{0,8},{8,16},{16,24},{24,32},{32,40},{40,48},{48,56},{56,64},{64,7... | collective-permute-start | bytes 98312 | tf_op jit(solution)/shard_map/while/body/eval_jaxpr/ppermute | solution.py:18
  58.1 1.3 collective-permute-start
  59.4 5.2 %collective-permute-start.1 = (f32[2,1,32,128]{3,2,1,0:T(8,128)S(1)}, f32[2,1,32,128]{3,2,1,0:T(8,128)S(1)}, u32[]{:S(2)}, u32[]{:S(2)}) collective-permute-start(f32[2,1,32,128]{3,2,1,0:T(8,128)S(1)} %get-tuple-element.226), channel_id=1, source_target_pairs={{0,8},{8,16},{16,24},{24,32},{32,40},{40,48},{48,56},{56,64},{64,7... | collective-permute-start | bytes 98312 | tf_op jit(solution)/shard_map/while/body/eval_jaxpr/ppermute | solution.py:18
  66.0 1.3 collective-permute-start
  67.3 5.3 %collective-permute-start.1 = (f32[2,1,32,128]{3,2,1,0:T(8,128)S(1)}, f32[2,1,32,128]{3,2,1,0:T(8,128)S(1)}, u32[]{:S(2)}, u32[]{:S(2)}) collective-permute-start(f32[2,1,32,128]{3,2,1,0:T(8,128)S(1)} %get-tuple-element.226), channel_id=1, source_target_pairs={{0,8},{8,16},{16,24},{24,32},{32,40},{40,48},{48,56},{56,64},{64,7... | collective-permute-start | bytes 98312 | tf_op jit(solution)/shard_map/while/body/eval_jaxpr/ppermute | solution.py:18
  74.1 1.3 collective-permute-start
  75.4 5.3 %collective-permute-start.1 = (f32[2,1,32,128]{3,2,1,0:T(8,128)S(1)}, f32[2,1,32,128]{3,2,1,0:T(8,128)S(1)}, u32[]{:S(2)}, u32[]{:S(2)}) collective-permute-start(f32[2,1,32,128]{3,2,1,0:T(8,128)S(1)} %get-tuple-element.226), channel_id=1, source_target_pairs={{0,8},{8,16},{16,24},{24,32},{32,40},{40,48},{48,56},{56,64},{64,7... | collective-permute-start | bytes 98312 | tf_op jit(solution)/shard_map/while/body/eval_jaxpr/ppermute | solution.py:18
  82.2 1.3 collective-permute-start
  83.5 5.2 %collective-permute-start.1 = (f32[2,1,32,128]{3,2,1,0:T(8,128)S(1)}, f32[2,1,32,128]{3,2,1,0:T(8,128)S(1)}, u32[]{:S(2)}, u32[]{:S(2)}) collective-permute-start(f32[2,1,32,128]{3,2,1,0:T(8,128)S(1)} %get-tuple-element.226), channel_id=1, source_target_pairs={{0,8},{8,16},{16,24},{24,32},{32,40},{40,48},{48,56},{56,64},{64,7... | collective-permute-start | bytes 98312 | tf_op jit(solution)/shard_map/while/body/eval_jaxpr/ppermute | solution.py:18
  90.2 1.3 collective-permute-start
  91.5 6.5 %collective-permute-start.1 = (f32[2,1,32,128]{3,2,1,0:T(8,128)S(1)}, f32[2,1,32,128]{3,2,1,0:T(8,128)S(1)}, u32[]{:S(2)}, u32[]{:S(2)}) collective-permute-start(f32[2,1,32,128]{3,2,1,0:T(8,128)S(1)} %get-tuple-element.226), channel_id=1, source_target_pairs={{0,8},{8,16},{16,24},{24,32},{32,40},{40,48},{48,56},{56,64},{64,7... | collective-permute-start | bytes 98312 | tf_op jit(solution)/shard_map/while/body/eval_jaxpr/ppermute | solution.py:18
  100.3 20.7 %all-to-all-start = ((f32[2,5,32,128]{3,0,1,2:T(2,128)}), f32[2,5,32,128]{3,0,1,2:T(2,128)S(1)}, u32[]{:S(2)}, u32[]{:S(2)}) async-start(f32[2,5,32,128]{3,0,1,2:T(2,128)} %copy.27), calls=%async_computation | async-start | bytes 327680 | tf_op jit(solution)/shard_map/all_to_all | solution.py:87
  121.2 8.6 %all-to-all-done = f32[2,5,32,128]{3,0,1,2:T(2,128)S(1)} async-done(((f32[2,5,32,128]{3,0,1,2:T(2,128)}), f32[2,5,32,128]{3,0,1,2:T(2,128)S(1)}, u32[]{:S(2)}, u32[]{:S(2)}) %all-to-all-start) | async-done | bytes 163872 | tf_op jit(solution)/shard_map/all_to_all | solution.py:87
  130.4 26.5 %while.23 = (s32[]{:T(128)}, f32[8,32,2560]{2,1,0:T(8,128)S(1)}, f32[8,32,16]{1,0,2:T(8,128)S(1)}, f32[8,32,16]{1,0,2:T(8,128)S(1)}, f32[16,5,4,128]{3,2,1,0:T(4...) while((s32[]{:T(128)}, f32[8,32,2560]{2,1,0:T(8,128)S(1)}, f32[8,32,16]{1,0,2:T(8,128)S(1)}, ...), condition=%wide.wide.region_7.8_spmd, body=%wide.wide.region_3.7_spmd.sunk | while | flops 10404322 | bytes 2648417 | solution.py:91
  130.6 1.2 fusion.17
  131.9 1.8 fusion.18
  133.9 1.2 fusion.17
  135.3 1.8 fusion.18
  137.2 1.2 fusion.17
  138.6 1.8 fusion.18
  140.6 1.2 fusion.17
  141.9 1.8 fusion.18
  143.9 1.2 fusion.17
  145.2 1.8 fusion.18
  147.2 1.2 fusion.17
  148.5 1.8 fusion.18
  151.8 1.8 fusion.18
  155.1 1.8 fusion.18
  157.3 141.2 %pmax.7 = f32[256]{0:T(256)S(1)} all-reduce(f32[256]{0:T(256)S(1)} %reduce_max.12), channel_id=1, replica_groups=mesh['space'=64,'sta'=8] {'space','sta'}, use_global_device_ids=true, to_apply=%region_9.10 | all-reduce | flops 256 | bytes 2048 | tf_op jit(solution)/shard_map/pmax | solution.py:97
  298.5 2.0 exponential_reduce_fusion
  300.5 2.8 div.34
  303.4 94.4 %psum.7 = f32[256]{0:T(256)S(1)} all-reduce(f32[256]{0:T(256)S(1)} %reduce_sum.49), channel_id=1, replica_groups=mesh['space'=64,'sta'=8] {'space','sta'}, use_global_device_ids=true, to_apply=%region_11.12 | all-reduce | flops 256 | bytes 2048 | tf_op jit(solution)/shard_map/psum | solution.py:99
  397.8 2.5 exponential_divide_fusion
  (165 shorter events, 25.0 us)
Async XLA Ops:
  3.1 117.9 %copy-start.2 = (s32[256,16]{0,1:T(8,128)S(1)}, s32[256,16]{0,1:T(8,128)}, u32[]{:S(2)}) copy-start(s32[256,16]{0,1:T(8,128)} %param.13) | copy-start | bytes 49156
  3.1 118.0 %copy-start.1 = (f32[256,16]{0,1:T(8,128)S(1)}, f32[256,16]{0,1:T(8,128)}, u32[]{:S(2)}) copy-start(f32[256,16]{0,1:T(8,128)} %param.12) | copy-start | bytes 49156
  3.1 6.0 %collective-permute-start = (f32[2,1,32,128]{3,2,1,0:T(8,128)S(1)}, f32[2,1,32,128]{3,2,1,0:T(8,128)S(1)}, u32[]{:S(2)}, u32[]{:S(2)}) collective-permute-start(f32[2,1,32,128]{3,2,1,0:T(8,128)S(1)} %get-tuple-element.225), channel_id=1, source_target_pairs={{8,0},{16,8},{24,16},{32,24},{40,32},{48,40},{56,48},{64,56},{72,6... | collective-permute-start | bytes 98312 | tf_op jit(solution)/shard_map/while/body/eval_jaxpr/ppermute | solution.py:21
  4.4 5.7 %collective-permute-start.1 = (f32[2,1,32,128]{3,2,1,0:T(8,128)S(1)}, f32[2,1,32,128]{3,2,1,0:T(8,128)S(1)}, u32[]{:S(2)}, u32[]{:S(2)}) collective-permute-start(f32[2,1,32,128]{3,2,1,0:T(8,128)S(1)} %get-tuple-element.226), channel_id=1, source_target_pairs={{0,8},{8,16},{16,24},{24,32},{32,40},{40,48},{48,56},{56,64},{64,7... | collective-permute-start | bytes 98312 | tf_op jit(solution)/shard_map/while/body/eval_jaxpr/ppermute | solution.py:18
  10.6 6.2 %collective-permute-start = (f32[2,1,32,128]{3,2,1,0:T(8,128)S(1)}, f32[2,1,32,128]{3,2,1,0:T(8,128)S(1)}, u32[]{:S(2)}, u32[]{:S(2)}) collective-permute-start(f32[2,1,32,128]{3,2,1,0:T(8,128)S(1)} %get-tuple-element.225), channel_id=1, source_target_pairs={{8,0},{16,8},{24,16},{32,24},{40,32},{48,40},{56,48},{64,56},{72,6... | collective-permute-start | bytes 98312 | tf_op jit(solution)/shard_map/while/body/eval_jaxpr/ppermute | solution.py:21
  11.9 5.9 %collective-permute-start.1 = (f32[2,1,32,128]{3,2,1,0:T(8,128)S(1)}, f32[2,1,32,128]{3,2,1,0:T(8,128)S(1)}, u32[]{:S(2)}, u32[]{:S(2)}) collective-permute-start(f32[2,1,32,128]{3,2,1,0:T(8,128)S(1)} %get-tuple-element.226), channel_id=1, source_target_pairs={{0,8},{8,16},{16,24},{24,32},{32,40},{40,48},{48,56},{56,64},{64,7... | collective-permute-start | bytes 98312 | tf_op jit(solution)/shard_map/while/body/eval_jaxpr/ppermute | solution.py:18
  18.2 6.5 %collective-permute-start = (f32[2,1,32,128]{3,2,1,0:T(8,128)S(1)}, f32[2,1,32,128]{3,2,1,0:T(8,128)S(1)}, u32[]{:S(2)}, u32[]{:S(2)}) collective-permute-start(f32[2,1,32,128]{3,2,1,0:T(8,128)S(1)} %get-tuple-element.225), channel_id=1, source_target_pairs={{8,0},{16,8},{24,16},{32,24},{40,32},{48,40},{56,48},{64,56},{72,6... | collective-permute-start | bytes 98312 | tf_op jit(solution)/shard_map/while/body/eval_jaxpr/ppermute | solution.py:21
  19.5 6.2 %collective-permute-start.1 = (f32[2,1,32,128]{3,2,1,0:T(8,128)S(1)}, f32[2,1,32,128]{3,2,1,0:T(8,128)S(1)}, u32[]{:S(2)}, u32[]{:S(2)}) collective-permute-start(f32[2,1,32,128]{3,2,1,0:T(8,128)S(1)} %get-tuple-element.226), channel_id=1, source_target_pairs={{0,8},{8,16},{16,24},{24,32},{32,40},{40,48},{48,56},{56,64},{64,7... | collective-permute-start | bytes 98312 | tf_op jit(solution)/shard_map/while/body/eval_jaxpr/ppermute | solution.py:18
  26.2 6.5 %collective-permute-start = (f32[2,1,32,128]{3,2,1,0:T(8,128)S(1)}, f32[2,1,32,128]{3,2,1,0:T(8,128)S(1)}, u32[]{:S(2)}, u32[]{:S(2)}) collective-permute-start(f32[2,1,32,128]{3,2,1,0:T(8,128)S(1)} %get-tuple-element.225), channel_id=1, source_target_pairs={{8,0},{16,8},{24,16},{32,24},{40,32},{48,40},{56,48},{64,56},{72,6... | collective-permute-start | bytes 98312 | tf_op jit(solution)/shard_map/while/body/eval_jaxpr/ppermute | solution.py:21
  27.5 6.2 %collective-permute-start.1 = (f32[2,1,32,128]{3,2,1,0:T(8,128)S(1)}, f32[2,1,32,128]{3,2,1,0:T(8,128)S(1)}, u32[]{:S(2)}, u32[]{:S(2)}) collective-permute-start(f32[2,1,32,128]{3,2,1,0:T(8,128)S(1)} %get-tuple-element.226), channel_id=1, source_target_pairs={{0,8},{8,16},{16,24},{24,32},{32,40},{40,48},{48,56},{56,64},{64,7... | collective-permute-start | bytes 98312 | tf_op jit(solution)/shard_map/while/body/eval_jaxpr/ppermute | solution.py:18
  34.2 6.5 %collective-permute-start = (f32[2,1,32,128]{3,2,1,0:T(8,128)S(1)}, f32[2,1,32,128]{3,2,1,0:T(8,128)S(1)}, u32[]{:S(2)}, u32[]{:S(2)}) collective-permute-start(f32[2,1,32,128]{3,2,1,0:T(8,128)S(1)} %get-tuple-element.225), channel_id=1, source_target_pairs={{8,0},{16,8},{24,16},{32,24},{40,32},{48,40},{56,48},{64,56},{72,6... | collective-permute-start | bytes 98312 | tf_op jit(solution)/shard_map/while/body/eval_jaxpr/ppermute | solution.py:21
  35.5 6.2 %collective-permute-start.1 = (f32[2,1,32,128]{3,2,1,0:T(8,128)S(1)}, f32[2,1,32,128]{3,2,1,0:T(8,128)S(1)}, u32[]{:S(2)}, u32[]{:S(2)}) collective-permute-start(f32[2,1,32,128]{3,2,1,0:T(8,128)S(1)} %get-tuple-element.226), channel_id=1, source_target_pairs={{0,8},{8,16},{16,24},{24,32},{32,40},{40,48},{48,56},{56,64},{64,7... | collective-permute-start | bytes 98312 | tf_op jit(solution)/shard_map/while/body/eval_jaxpr/ppermute | solution.py:18
  42.1 6.5 %collective-permute-start = (f32[2,1,32,128]{3,2,1,0:T(8,128)S(1)}, f32[2,1,32,128]{3,2,1,0:T(8,128)S(1)}, u32[]{:S(2)}, u32[]{:S(2)}) collective-permute-start(f32[2,1,32,128]{3,2,1,0:T(8,128)S(1)} %get-tuple-element.225), channel_id=1, source_target_pairs={{8,0},{16,8},{24,16},{32,24},{40,32},{48,40},{56,48},{64,56},{72,6... | collective-permute-start | bytes 98312 | tf_op jit(solution)/shard_map/while/body/eval_jaxpr/ppermute | solution.py:21
  43.4 6.2 %collective-permute-start.1 = (f32[2,1,32,128]{3,2,1,0:T(8,128)S(1)}, f32[2,1,32,128]{3,2,1,0:T(8,128)S(1)}, u32[]{:S(2)}, u32[]{:S(2)}) collective-permute-start(f32[2,1,32,128]{3,2,1,0:T(8,128)S(1)} %get-tuple-element.226), channel_id=1, source_target_pairs={{0,8},{8,16},{16,24},{24,32},{32,40},{40,48},{48,56},{56,64},{64,7... | collective-permute-start | bytes 98312 | tf_op jit(solution)/shard_map/while/body/eval_jaxpr/ppermute | solution.py:18
  50.1 6.5 %collective-permute-start = (f32[2,1,32,128]{3,2,1,0:T(8,128)S(1)}, f32[2,1,32,128]{3,2,1,0:T(8,128)S(1)}, u32[]{:S(2)}, u32[]{:S(2)}) collective-permute-start(f32[2,1,32,128]{3,2,1,0:T(8,128)S(1)} %get-tuple-element.225), channel_id=1, source_target_pairs={{8,0},{16,8},{24,16},{32,24},{40,32},{48,40},{56,48},{64,56},{72,6... | collective-permute-start | bytes 98312 | tf_op jit(solution)/shard_map/while/body/eval_jaxpr/ppermute | solution.py:21
  51.4 6.2 %collective-permute-start.1 = (f32[2,1,32,128]{3,2,1,0:T(8,128)S(1)}, f32[2,1,32,128]{3,2,1,0:T(8,128)S(1)}, u32[]{:S(2)}, u32[]{:S(2)}) collective-permute-start(f32[2,1,32,128]{3,2,1,0:T(8,128)S(1)} %get-tuple-element.226), channel_id=1, source_target_pairs={{0,8},{8,16},{16,24},{24,32},{32,40},{40,48},{48,56},{56,64},{64,7... | collective-permute-start | bytes 98312 | tf_op jit(solution)/shard_map/while/body/eval_jaxpr/ppermute | solution.py:18
  58.1 6.5 %collective-permute-start = (f32[2,1,32,128]{3,2,1,0:T(8,128)S(1)}, f32[2,1,32,128]{3,2,1,0:T(8,128)S(1)}, u32[]{:S(2)}, u32[]{:S(2)}) collective-permute-start(f32[2,1,32,128]{3,2,1,0:T(8,128)S(1)} %get-tuple-element.225), channel_id=1, source_target_pairs={{8,0},{16,8},{24,16},{32,24},{40,32},{48,40},{56,48},{64,56},{72,6... | collective-permute-start | bytes 98312 | tf_op jit(solution)/shard_map/while/body/eval_jaxpr/ppermute | solution.py:21
  59.4 6.2 %collective-permute-start.1 = (f32[2,1,32,128]{3,2,1,0:T(8,128)S(1)}, f32[2,1,32,128]{3,2,1,0:T(8,128)S(1)}, u32[]{:S(2)}, u32[]{:S(2)}) collective-permute-start(f32[2,1,32,128]{3,2,1,0:T(8,128)S(1)} %get-tuple-element.226), channel_id=1, source_target_pairs={{0,8},{8,16},{16,24},{24,32},{32,40},{40,48},{48,56},{56,64},{64,7... | collective-permute-start | bytes 98312 | tf_op jit(solution)/shard_map/while/body/eval_jaxpr/ppermute | solution.py:18
  66.0 6.6 %collective-permute-start = (f32[2,1,32,128]{3,2,1,0:T(8,128)S(1)}, f32[2,1,32,128]{3,2,1,0:T(8,128)S(1)}, u32[]{:S(2)}, u32[]{:S(2)}) collective-permute-start(f32[2,1,32,128]{3,2,1,0:T(8,128)S(1)} %get-tuple-element.225), channel_id=1, source_target_pairs={{8,0},{16,8},{24,16},{32,24},{40,32},{48,40},{56,48},{64,56},{72,6... | collective-permute-start | bytes 98312 | tf_op jit(solution)/shard_map/while/body/eval_jaxpr/ppermute | solution.py:21
  67.3 6.3 %collective-permute-start.1 = (f32[2,1,32,128]{3,2,1,0:T(8,128)S(1)}, f32[2,1,32,128]{3,2,1,0:T(8,128)S(1)}, u32[]{:S(2)}, u32[]{:S(2)}) collective-permute-start(f32[2,1,32,128]{3,2,1,0:T(8,128)S(1)} %get-tuple-element.226), channel_id=1, source_target_pairs={{0,8},{8,16},{16,24},{24,32},{32,40},{40,48},{48,56},{56,64},{64,7... | collective-permute-start | bytes 98312 | tf_op jit(solution)/shard_map/while/body/eval_jaxpr/ppermute | solution.py:18
  74.1 6.7 %collective-permute-start = (f32[2,1,32,128]{3,2,1,0:T(8,128)S(1)}, f32[2,1,32,128]{3,2,1,0:T(8,128)S(1)}, u32[]{:S(2)}, u32[]{:S(2)}) collective-permute-start(f32[2,1,32,128]{3,2,1,0:T(8,128)S(1)} %get-tuple-element.225), channel_id=1, source_target_pairs={{8,0},{16,8},{24,16},{32,24},{40,32},{48,40},{56,48},{64,56},{72,6... | collective-permute-start | bytes 98312 | tf_op jit(solution)/shard_map/while/body/eval_jaxpr/ppermute | solution.py:21
  75.4 6.4 %collective-permute-start.1 = (f32[2,1,32,128]{3,2,1,0:T(8,128)S(1)}, f32[2,1,32,128]{3,2,1,0:T(8,128)S(1)}, u32[]{:S(2)}, u32[]{:S(2)}) collective-permute-start(f32[2,1,32,128]{3,2,1,0:T(8,128)S(1)} %get-tuple-element.226), channel_id=1, source_target_pairs={{0,8},{8,16},{16,24},{24,32},{32,40},{40,48},{48,56},{56,64},{64,7... | collective-permute-start | bytes 98312 | tf_op jit(solution)/shard_map/while/body/eval_jaxpr/ppermute | solution.py:18
  82.2 6.5 %collective-permute-start = (f32[2,1,32,128]{3,2,1,0:T(8,128)S(1)}, f32[2,1,32,128]{3,2,1,0:T(8,128)S(1)}, u32[]{:S(2)}, u32[]{:S(2)}) collective-permute-start(f32[2,1,32,128]{3,2,1,0:T(8,128)S(1)} %get-tuple-element.225), channel_id=1, source_target_pairs={{8,0},{16,8},{24,16},{32,24},{40,32},{48,40},{56,48},{64,56},{72,6... | collective-permute-start | bytes 98312 | tf_op jit(solution)/shard_map/while/body/eval_jaxpr/ppermute | solution.py:21
  83.5 6.2 %collective-permute-start.1 = (f32[2,1,32,128]{3,2,1,0:T(8,128)S(1)}, f32[2,1,32,128]{3,2,1,0:T(8,128)S(1)}, u32[]{:S(2)}, u32[]{:S(2)}) collective-permute-start(f32[2,1,32,128]{3,2,1,0:T(8,128)S(1)} %get-tuple-element.226), channel_id=1, source_target_pairs={{0,8},{8,16},{16,24},{24,32},{32,40},{40,48},{48,56},{56,64},{64,7... | collective-permute-start | bytes 98312 | tf_op jit(solution)/shard_map/while/body/eval_jaxpr/ppermute | solution.py:18
  90.2 7.9 %collective-permute-start = (f32[2,1,32,128]{3,2,1,0:T(8,128)S(1)}, f32[2,1,32,128]{3,2,1,0:T(8,128)S(1)}, u32[]{:S(2)}, u32[]{:S(2)}) collective-permute-start(f32[2,1,32,128]{3,2,1,0:T(8,128)S(1)} %get-tuple-element.225), channel_id=1, source_target_pairs={{8,0},{16,8},{24,16},{32,24},{40,32},{48,40},{56,48},{64,56},{72,6... | collective-permute-start | bytes 98312 | tf_op jit(solution)/shard_map/while/body/eval_jaxpr/ppermute | solution.py:21
  91.5 7.5 %collective-permute-start.1 = (f32[2,1,32,128]{3,2,1,0:T(8,128)S(1)}, f32[2,1,32,128]{3,2,1,0:T(8,128)S(1)}, u32[]{:S(2)}, u32[]{:S(2)}) collective-permute-start(f32[2,1,32,128]{3,2,1,0:T(8,128)S(1)} %get-tuple-element.226), channel_id=1, source_target_pairs={{0,8},{8,16},{16,24},{24,32},{32,40},{40,48},{48,56},{56,64},{64,7... | collective-permute-start | bytes 98312 | tf_op jit(solution)/shard_map/while/body/eval_jaxpr/ppermute | solution.py:18
  100.3 29.5 %all-to-all-start = ((f32[2,5,32,128]{3,0,1,2:T(2,128)}), f32[2,5,32,128]{3,0,1,2:T(2,128)S(1)}, u32[]{:S(2)}, u32[]{:S(2)}) async-start(f32[2,5,32,128]{3,0,1,2:T(2,128)} %copy.27), calls=%async_computation | async-start | bytes 327680 | tf_op jit(solution)/shard_map/all_to_all | solution.py:87
  129.8 0.7 copy-start
where the time goes:
time: 401 us; the launch traced here: 400 us
  blocking collectives  236 us (59%)
  starting transfers between devices  99.1 us (25%)
  other arithmetic  36.1 us (9%)
  waiting for transfers between devices  20.1 us (5%)
  local copies, waits for them, and re-layouts  7.41 us (2%)
    pmax x1, blocking collectives, body(): top_score = lax.pmax(local_top, ('space', 'sta'))  141 us
    psum x1, blocking collectives, body(): mass_sum = lax.psum(jnp.sum(cell_weights, 1), ('space', 'sta'))  94.4 us
    ppermute x12, starting transfers between devices, extended_2(): lax.ppermute(lax.slice_in_dim(block, block.shape[dim] - width, None, axis...  62.9 us
    all_to_all x1, starting transfers between devices, body(): lax.all_to_all(tables, 'sta', split_axis=2, concat_axis=0, tiled=True)  20.7 us
    ppermute x12, starting transfers between devices, extended_2(): lax.ppermute(lax.slice_in_dim(block, 0, width, axis=dim), axis, backward)  15.5 us
    reduce_sum x8, other arithmetic, misfit_block(): return jnp.sum(observed[:, :, None] * deviation * deviation, 1)  14 us
    ppermute x12, waiting for transfers between devices, extended_2(): lax.ppermute(lax.slice_in_dim(block, block.shape[dim] - width, None, axis...  11.5 us
    reduce_sum x8, other arithmetic, misfit_block(): jnp.sum(observed[:, :, None] * residual, 1) / pick_count[:, None]  9.54 us
  transfers between devices with their start and end apart: 25, of which 13 were waited for; matrix products, arithmetic and copies ran while one was open for 0% of the time, Pallas kernels for 0%

commit v1 on v0

--- a/solution.py
+++ b/solution.py
@@ -96,7 +96,11 @@
     local_top = jnp.max(score, 1)
     top_score = lax.pmax(local_top, ("space", "sta"))
     cell_weights = jnp.exp(score - top_score[:, None])
-    mass_sum = lax.psum(jnp.sum(cell_weights, 1), ("space", "sta"))
+
+    def register_pipes_on_mesh(xx):
+        return jax.lax.all_gather(xx, ("space", "sta")).sum(axis=0)
+
+    mass_sum = register_pipes_on_mesh(jnp.sum(cell_weights, 1))
     density = cell_weights / mass_sum[:, None]
     density = density.reshape(picks.shape[0], refined.shape[1], refined.shape[2], refined.shape[3])
     return (refined, density)

time: 401 us -> 989 us (2.47)
  blocking collectives: 236 us -> 823 us
    all_gather x0 -> x1, blocking collectives: none -> 681 us  [register_pipes_on_mesh(): return jax.lax.all_gather(xx, ('space', 'sta')).sum(axis=0)]
    psum x1 -> x0, blocking collectives: 94.4 us -> none  [body(): mass_sum = lax.psum(jnp.sum(cell_weights, 1), ('space', 'sta'))]
where the time goes in v1:
time: 989 us; the launch traced here: 988 us
  blocking collectives  823 us (83%)
  starting transfers between devices  99.1 us (10%)
  other arithmetic  36.7 us (4%)
  waiting for transfers between devices  20.1 us (2%)
    all_gather x1, blocking collectives, register_pipes_on_mesh(): return jax.lax.all_gather(xx, ('space', 'sta')).sum(axis=0)  681 us
    pmax x1, blocking collectives, body(): top_score = lax.pmax(local_top, ('space', 'sta'))  141 us
    ppermute x12, starting transfers between devices, extended_2(): lax.ppermute(lax.slice_in_dim(block, block.shape[dim] - width, None, axis...  62.9 us
    all_to_all x1, starting transfers between devices, body(): lax.all_to_all(tables, 'sta', split_axis=2, concat_axis=0, tiled=True)  20.7 us
  transfers between devices with their start and end apart: 25, of which 13 were waited for; matrix products, arithmetic and copies ran while one was open for 0% of the time, Pallas kernels for 0%

profile of v1, /device:TPU:1, one launch (start us, length us, event | category | flops | bytes accessed | tf_op | source)
XLA Modules:
  0.0 987.9 jit_solution(10884797477162262183)
XLA Ops:
  1.5 1.5 select_reduce_fusion
  3.1 96.4 %while.22 = (s32[]{:T(128)}, f32[2,5,32,128]{3,2,1,0:T(8,128)S(1)}, pred[]{:T(512)}, pred[]{:T(512)}, f32[5,32,128]{2,1,0:T(8,128)S(1)}, /*index=5*/f32[1,5,32,128]{3,2,1,0:T(8,128)S(1)}, s32[]{:T(128)}) while((s32[]{:T(128)}, f32[2,5,32,128]{3,2,1,0:T(8,128)S(1)}, pred[]{:T(512)}, pred[]{:T(512)}, f32[5,32,128]{2,1,0:T(8,128)S(1)}, ...), condition=%wide.region_2.3_spmd, body=%wide.region_1.2_spmd.sunk | while | flops 1523749 | bytes 2244781 | solution.py:86
  3.1 1.3 collective-permute-start
  4.4 4.6 collective-permute-start.1
  10.6 1.3 collective-permute-start
  11.9 4.9 collective-permute-start.1
  18.2 1.3 collective-permute-start
  19.5 5.2 collective-permute-start.1
  26.2 1.3 collective-permute-start
  27.5 5.2 collective-permute-start.1
  34.2 1.3 collective-permute-start
  35.5 5.2 collective-permute-start.1
  42.1 1.3 collective-permute-start
  43.4 5.2 collective-permute-start.1
  50.1 1.3 collective-permute-start
  51.4 5.2 collective-permute-start.1
  58.1 1.3 collective-permute-start
  59.4 5.2 collective-permute-start.1
  66.0 1.3 collective-permute-start
  67.3 5.3 collective-permute-start.1
  74.1 1.3 collective-permute-start
  75.4 5.3 collective-permute-start.1
  82.2 1.3 collective-permute-start
  83.5 5.2 collective-permute-start.1
  90.2 1.3 collective-permute-start
  91.5 6.5 collective-permute-start.1
  100.3 20.7 %all-to-all-start = ((f32[2,5,32,128]{3,0,1,2:T(2,128)}), f32[2,5,32,128]{3,0,1,2:T(2,128)S(1)}, u32[]{:S(2)}, u32[]{:S(2)}) async-start(f32[2,5,32,128]{3,0,1,2:T(2,128)} %copy.27), calls=%async_computation | async-start | bytes 327680 | tf_op jit(solution)/shard_map/all_to_all | solution.py:87
  121.2 8.6 all-to-all-done
  130.4 26.5 %while.23 = (s32[]{:T(128)}, f32[8,32,2560]{2,1,0:T(8,128)S(1)}, f32[8,32,16]{1,0,2:T(8,128)S(1)}, f32[8,32,16]{1,0,2:T(8,128)S(1)}, f32[16,5,4,128]{3,2,1,0:T(4...) while((s32[]{:T(128)}, f32[8,32,2560]{2,1,0:T(8,128)S(1)}, f32[8,32,16]{1,0,2:T(8,128)S(1)}, ...), condition=%wide.wide.region_7.8_spmd, body=%wide.wide.region_3.7_spmd.sunk | while | flops 10404322 | bytes 2648417 | solution.py:91
  130.6 1.2 fusion.17
  131.9 1.8 fusion.18
  133.9 1.2 fusion.17
  135.3 1.8 fusion.18
  137.2 1.2 fusion.17
  138.6 1.8 fusion.18
  140.6 1.2 fusion.17
  141.9 1.8 fusion.18
  143.9 1.2 fusion.17
  145.2 1.8 fusion.18
  147.2 1.2 fusion.17
  148.5 1.8 fusion.18
  151.8 1.8 fusion.18
  155.1 1.8 fusion.18
  157.3 141.2 %pmax.7 = f32[256]{0:T(256)S(1)} all-reduce(f32[256]{0:T(256)S(1)} %reduce_max.12), channel_id=1, replica_groups=mesh['space'=64,'sta'=8] {'space','sta'}, use_global_device_ids=true, to_apply=%region_9.10 | all-reduce | flops 256 | bytes 2048 | tf_op jit(solution)/shard_map/pmax | solution.py:97
  298.5 2.0 exponential_reduce_fusion
  300.5 2.8 div.34
  303.4 681.3 %all-gather = f32[512,1,256]{2,1,0:T(1,128)S(1)} all-gather(f32[1,1,256]{2,1,0:T(1,128)S(1)} %reshape.91), channel_id=1, replica_groups=mesh['space'=64,'sta'=8] {'space','sta'}, dimensions={0}, use_global_device_ids=true | all-gather | bytes 525312 | tf_op jit(solution)/shard_map/all_gather | solution.py:101
  985.3 2.6 exponential_divide_fusion
  (166 shorter events, 25.6 us)
Async XLA Ops:
  3.1 117.9 %copy-start.2 = (s32[256,16]{0,1:T(8,128)S(1)}, s32[256,16]{0,1:T(8,128)}, u32[]{:S(2)}) copy-start(s32[256,16]{0,1:T(8,128)} %param.13) | copy-start | bytes 49156
  3.1 118.0 %copy-start.1 = (f32[256,16]{0,1:T(8,128)S(1)}, f32[256,16]{0,1:T(8,128)}, u32[]{:S(2)}) copy-start(f32[256,16]{0,1:T(8,128)} %param.12) | copy-start | bytes 49156
  3.1 6.0 collective-permute-start
  4.4 5.7 collective-permute-start.1
  10.6 6.2 collective-permute-start
  11.9 5.9 collective-permute-start.1
  18.2 6.5 collective-permute-start
  19.5 6.2 collective-permute-start.1
  26.2 6.5 collective-permute-start
  27.5 6.2 collective-permute-start.1
  34.2 6.5 collective-permute-start
  35.5 6.2 collective-permute-start.1
  42.1 6.5 collective-permute-start
  43.4 6.2 collective-permute-start.1
  50.1 6.5 collective-permute-start
  51.4 6.2 collective-permute-start.1
  58.1 6.5 collective-permute-start
  59.4 6.2 collective-permute-start.1
  66.0 6.6 collective-permute-start
  67.3 6.3 collective-permute-start.1
  74.1 6.7 collective-permute-start
  75.4 6.4 collective-permute-start.1
  82.2 6.5 collective-permute-start
  83.5 6.2 collective-permute-start.1
  90.2 7.9 collective-permute-start
  91.5 7.5 collective-permute-start.1
  100.3 29.5 %all-to-all-start = ((f32[2,5,32,128]{3,0,1,2:T(2,128)}), f32[2,5,32,128]{3,0,1,2:T(2,128)S(1)}, u32[]{:S(2)}, u32[]{:S(2)}) async-start(f32[2,5,32,128]{3,0,1,2:T(2,128)} %copy.27), calls=%async_computation | async-start | bytes 327680 | tf_op jit(solution)/shard_map/all_to_all | solution.py:87
  129.8 0.7 copy-start
